TPU v7x, 32 devices: a whole 2x2x4 slice. The times are simulated.
32 devices in a mesh: dp: 16 (over z, y, core), ctx: 2 (over x).
Axes of the slice: x: 2, y: 2, z: 4, core: 2. Of those that a mesh axis runs over, the one named last changes fastest.
Arguments:
- conv_input: bfloat16 [16, 256, 4096], P('dp', 'ctx'), may hold values from -6 to 6
- gate_value: bfloat16 [16, 256, 4096], P('dp', 'ctx'), may hold values from -6 to 6
- out_grad: bfloat16 [16, 256, 4096], P('dp', 'ctx'), may hold values from -6 to 6
- filter_taps: bfloat16 [128, 4096], P('dp'), may hold values from -0.5 to 0.5
Outputs:
- input_grad: bfloat16 [16, 256, 4096], P('dp', 'ctx')
- filter_grad: float32 [128, 4096], P('dp')
All inputs are finite; a program needn't handle non-finite values.
Results may differ from a plain program's by a relative error of at most 0.0051.
Values may be sent and summed in bfloat16 or wider, within the bound.
A program may use at most 64 MiB of HBM per device.

v0:
```python
import functools
import math

import jax
import jax.numpy as jnp
import numpy as np
from jax import lax
from jax.experimental import pallas as pl
from jax.experimental.pallas import tpu as pltpu
from jax.sharding import PartitionSpec as P


def split(values):
    high = values.astype(jnp.bfloat16)
    return high, (values - high.astype(np.float32)).astype(jnp.bfloat16)


def transforms(length):
    half = length // 2
    angle = np.pi * np.outer(2 * np.arange(half) + 1, np.arange(length)) / length
    forward = np.concatenate([np.cos(angle), -np.sin(angle)], 0)
    inverse = np.concatenate([np.cos(angle), -np.sin(angle)], 0).T / half
    return split(forward.astype(np.float32)), split(inverse.astype(np.float32))


def dot(a, b):
    return lax.dot_general(a, b, (((1,), (0,)), ((), ())), preferred_element_type=jnp.float32)


def general(conv_input, gate_value, out_grad, filter_taps):
    inputs = conv_input[0]
    rows = inputs.shape[0]
    taps = filter_taps.shape[0] * lax.axis_size("dp")
    (fh, fl), (bh, bl) = transforms(rows + taps)
    half = (rows + taps) // 2
    mixed = (out_grad[0].astype(jnp.float32) * gate_value[0].astype(jnp.float32)).astype(
        jnp.bfloat16
    )
    devices = lax.axis_size("ctx")
    rim = lax.ppermute(mixed[:taps], "ctx", [(i + 1, i) for i in range(devices - 1)])
    full_taps = lax.all_gather(filter_taps, "dp", axis=0, tiled=True)

    def spectrum(x, first=0):
        n = x.shape[0]
        s = dot(fh[:, first : first + n], x) + dot(fl[:, first : first + n], x)
        return s[:half], s[half:]

    def back(re, im, n):
        s = jnp.concatenate([re, im], 0)
        high = s.astype(jnp.bfloat16)
        low = (s - high.astype(jnp.float32)).astype(jnp.bfloat16)
        return dot(bh[:n], high) + dot(bl[:n], high) + dot(bh[:n], low)

    xr, xi = spectrum(inputs)
    gr0, gi0 = spectrum(mixed)
    gr1, gi1 = spectrum(rim, rows)
    gr, gi = gr0 + gr1, gi0 + gi1
    partial = back(xr * gr + xi * gi, xr * gi - xi * gr, taps)
    hr, hi = spectrum(full_taps)
    grad = back(hr * gr + hi * gi, hr * gi - hi * gr, rows)
    shard_grad = lax.psum(lax.psum_scatter(partial, "dp", scatter_dimension=0, tiled=True), "ctx")
    tokens_all = rows * devices * lax.axis_size("dp")
    return (grad.astype(jnp.bfloat16)[None], shard_grad * (1.0 / math.sqrt(tokens_all)))


CHUNKS = 8
MESH = pl.DeviceIdType.MESH


def kernel(
    pairs, ranks, scale,
    in_hbm, gate_hbm, cot_hbm, taps_hbm, f_hbm, b_hbm,
    obuf, fbuf,
    x_gate, x_cot, x_ext, g_ext, taps_all, f_all, b_all, p32, own32, csrc, cbuf, half32, ysrc, ybuf,
    zsrc, zbuf, xbuf,
    ld_in, ld_gate, ld_cot, ld_taps, ld_f,
    rim_s, rim_r, in_s, in_r, tz_s, ty_s, tc_s, tap_r,
    c_s, c_r, y_s, y_r, z_s, z_r, x_s, x_r,
):
    dp, ctx = lax.axis_index("dp"), lax.axis_index("ctx")
    core, mine = lax.rem(dp, 2), dp // 2
    partner = dp + 1 - 2 * core
    side, place, places = lax.rem(mine, 2), mine // 2, pairs // 2
    across = 2 * (mine + 1 - 2 * side) + core
    rows, channels = x_gate.shape
    wide = channels // CHUNKS
    middle = CHUNKS // 2
    last, first = ctx == ranks - 1, ctx == 0
    left, right = lax.max(ctx - 1, 0), lax.min(ctx + 1, ranks - 1)
    upper, lower = pl.ds(0, rows), pl.ds(rows, rows)

    def cols(c):
        return pl.ds(pl.multiple_of(c * wide, wide), wide)

    def load(src, dst, sem, c):
        return pltpu.make_async_copy(src.at[:, cols(c)], dst.at[:, cols(c)], sem.at[c])

    def load_in(c):
        return pltpu.make_async_copy(in_hbm.at[:, cols(c)], x_ext.at[lower, cols(c)], ld_in.at[c])

    def each(n, body, start=0):
        lax.fori_loop(start, n, lambda i, z: (body(i), z)[1], 0)

    own_taps = pltpu.make_async_copy(taps_hbm, taps_all.at[dp], ld_taps)
    load_f = pltpu.make_async_copy(f_hbm, f_all, ld_f.at[0])
    load_b = pltpu.make_async_copy(b_hbm, b_all, ld_f.at[1])

    def loads(c):
        load(cot_hbm, x_cot, ld_cot, c).start()
        load(gate_hbm, x_gate, ld_gate, c).start()

    each(CHUNKS, loads)
    own_taps.start()
    load_f.start()
    load_b.start()
    each(CHUNKS, lambda c: load_in(c).start())

    def z_peer(k):
        return lax.rem(place + k, places)

    def z_device(k):
        return 4 * z_peer(k) + 2 * side + core

    def rank(k):
        return lax.rem(ctx + k, ranks)

    barrier = pltpu.get_barrier_semaphore()
    pl.semaphore_signal(barrier, inc=1, device_id=(partner, ctx), device_id_type=MESH)
    pl.semaphore_signal(barrier, inc=1, device_id=(across, ctx), device_id_type=MESH)
    for k in range(1, places):
        pl.semaphore_signal(barrier, inc=1, device_id=(z_device(k), ctx), device_id_type=MESH)
    for k in range(1, ranks):
        pl.semaphore_signal(barrier, inc=1, device_id=(dp, rank(k)), device_id_type=MESH)
    def remote(src, dst, send, recv, to):
        return pltpu.make_async_remote_copy(
            src_ref=src, dst_ref=dst, send_sem=send, recv_sem=recv, device_id=to, device_id_type=MESH
        )

    def rim(c):
        return remote(g_ext.at[upper, cols(c)], g_ext.at[lower, cols(c)], rim_s.at[c], rim_r.at[c], (dp, left))

    def lend(c):
        return remote(in_hbm.at[:, cols(c)], x_ext.at[upper, cols(c)], in_s.at[c], in_r.at[c], (dp, right))

    def mix(c):
        load(cot_hbm, x_cot, ld_cot, c).wait()
        load(gate_hbm, x_gate, ld_gate, c).wait()
        a = x_cot[:, cols(c)].astype(jnp.float32)
        b = x_gate[:, cols(c)].astype(jnp.float32)
        g_ext[upper, cols(c)] = (a * b).astype(jnp.bfloat16)

    each(middle, mix)
    pl.semaphore_wait(barrier, places + ranks)

    def send_rim(c):
        @pl.when(ctx > 0)
        def _():
            rim(c).start()

    each(middle, send_rim)

    @pl.when(jnp.logical_not(last))
    def _():
        each(CHUNKS, lambda c: lend(c).start(), middle)

    each(CHUNKS, lambda c: (mix(c), send_rim(c)), middle)

    def shard(p, s, c):
        return taps_all.at[4 * p + 2 * s + c]

    def tap(p, s, c, sem, to):
        return remote(shard(p, s, c), shard(p, s, c), sem, tap_r.at[4 * p + 2 * s + c], (to, ctx))

    def tap_z(k):
        return tap(place, side, core, tz_s.at[k], z_device(k))

    def tap_y(p):
        return tap(p, side, core, ty_s.at[p], across)

    def tap_c(p, s):
        return tap(p, s, core, tc_s.at[p, s], partner)

    def tap_wait(p, s, c):
        tap(p, s, c, ty_s.at[p], partner).wait_recv()

    own_taps.wait()
    each(places, lambda k: tap_z(k).start(), 1)
    tap_y(place).start()
    tap_c(place, side).start()

    def pass_y():
        def one(k):
            tap_wait(z_peer(k), side, core)
            tap_y(z_peer(k)).start()
            tap_c(z_peer(k), side).start()

        each(places, one, 1)

    def pass_c():
        def one(p):
            tap_wait(p, 1 - side, core)
            tap_c(p, 1 - side).start()

        each(places, one)

    def all_taps():
        def one(p):
            tap_wait(p, 0, 1 - core)
            tap_wait(p, 1, 1 - core)

        each(places, one)

    @pl.when(last)
    def _():
        g_ext[lower, :] = jnp.zeros((rows, channels), jnp.bfloat16)

    @pl.when(first)
    def _():
        x_ext[upper, :] = jnp.zeros((rows, channels), jnp.bfloat16)

    load_f.wait()
    load_b.wait()

    def ahead(x):
        n = x.shape[0]
        return dot(f_all[0, :, :n], x) + dot(f_all[1, :, :n], x)

    def later(x):
        return dot(f_all[0, :, rows:], x) + dot(f_all[1, :, rows:], x)

    def back(value, n):
        high = value.astype(jnp.bfloat16)
        low = (value - high.astype(jnp.float32)).astype(jnp.bfloat16)
        return dot(b_all[0, :n, :], high) + dot(b_all[1, :n, :], high) + dot(b_all[0, :n, :], low)

    half = f_all.shape[1] // 2

    def correlate(a, g, n):
        ar, ai, gr, gi = a[:half], a[half:], g[:half], g[half:]
        return back(jnp.concatenate([ar * gr + ai * gi, ar * gi - ai * gr], 0), n)

    count = taps_all.shape[1]
    taps = 2 * pairs * count
    f32, bf = jnp.float32, jnp.bfloat16

    def chunk(i):
        return jnp.where(last, i, lax.rem(i + middle, CHUNKS))

    def cross(c):
        return remote(csrc.at[:, :, cols(c)], cbuf.at[:, :, cols(c)], c_s.at[c], c_r.at[c], (partner, ctx))

    def turn(c):
        return remote(ysrc.at[:, :, cols(c)], ybuf.at[:, :, cols(c)], y_s.at[c], y_r.at[c], (across, ctx))

    def spread(c, k):
        return remote(
            zsrc.at[z_peer(k), :, cols(c)], zbuf.at[place, :, cols(c)],
            z_s.at[k, c], z_r.at[place, c], (z_device(k), ctx),
        )

    def gathered(c, k):
        slot = zbuf.at[z_peer(k), :, cols(c)]
        return remote(slot, slot, z_s.at[k, c], z_r.at[z_peer(k), c], (z_device(k), ctx))

    def swap(c, k):
        slot = xbuf.at[ctx, :, cols(c)]
        return remote(slot, slot, x_s.at[k, c], x_r.at[ctx, c], (dp, rank(k)))

    def swapped(c, k):
        slot = xbuf.at[rank(k), :, cols(c)]
        return remote(slot, slot, x_s.at[k, c], x_r.at[rank(k), c], (dp, rank(k)))

    def stage1(c):
        load_in(c).wait()

        @pl.when(c < middle)
        def _():
            @pl.when(jnp.logical_not(last))
            def _():
                rim(c).wait_recv()

            p = correlate(ahead(x_ext[lower, cols(c)]), ahead(g_ext[:, cols(c)]), taps)
            p32[...] = p.reshape(places, 2, 2, count, wide)

        @pl.when(c >= middle)
        def _():
            @pl.when(jnp.logical_not(first))
            def _():
                lend(c).wait_recv()

            p = correlate(ahead(x_ext[:, cols(c)]), later(g_ext[upper, cols(c)]), taps)
            p32[...] = p.reshape(places, 2, 2, count, wide)

        for s in range(2):
            csrc[pl.ds(s * places, places), :, cols(c)] = p32[:, s, 1 - core].astype(bf)
            own32[pl.ds(s * places, places), :, cols(c)] = p32[:, s, core]
        cross(c).start()

    def stage2(c):
        cross(c).wait_recv()
        there, here = pl.ds((1 - side) * places, places), pl.ds(side * places, places)
        ysrc[:, :, cols(c)] = (own32[there, :, cols(c)] + cbuf[there, :, cols(c)].astype(f32)).astype(bf)
        turn(c).start()
        half32[:, :, cols(c)] = own32[here, :, cols(c)] + cbuf[here, :, cols(c)].astype(f32)

    def stage3(c):
        turn(c).wait_recv()
        total = half32[:, :, cols(c)] + ybuf[:, :, cols(c)].astype(f32)
        half32[:, :, cols(c)] = total
        zsrc[:, :, cols(c)] = total.astype(bf)
        for k in range(1, places):
            spread(c, k).start()

    def stage4(c):
        total = half32[place, :, cols(c)]
        for k in range(1, places):
            gathered(c, k).wait_recv()
            total = total + zbuf[z_peer(k), :, cols(c)].astype(f32)
        xbuf[ctx, :, cols(c)] = total.astype(bf)
        for k in range(1, ranks):
            swap(c, k).start()

    def finish(c):
        for k in range(1, ranks):
            swapped(c, k).wait_recv()
        total = xbuf[0, :, cols(c)].astype(f32)
        for r in range(1, ranks):
            total = total + xbuf[r, :, cols(c)].astype(f32)
        fbuf[:, cols(c)] = total * scale

    def grad(c):
        @pl.when(jnp.logical_and(c >= middle, jnp.logical_not(last)))
        def _():
            rim(c).wait_recv()

        t = taps_all[:, :, cols(c)].astype(f32).reshape(taps, wide).astype(bf)
        obuf[:, cols(c)] = correlate(ahead(t), ahead(g_ext[:, cols(c)]), rows).astype(bf)

    def step(i):
        for lag, stage in list(zip((0, 1, 3, 5), (stage1, stage2, stage3, stage4))):
            @pl.when(jnp.logical_and(i >= lag, i < CHUNKS + lag))
            def _(lag=lag, stage=stage):
                stage(chunk(i - lag))

        for when, action in ((2, pass_y), (middle + 1, pass_c), (CHUNKS - 1, all_taps)):
            @pl.when(i == when)
            def _(action=action):
                action()

        @pl.when(i >= CHUNKS - 1)
        def _():
            grad(i - CHUNKS + 1)

        @pl.when(i == 2 * CHUNKS - 2)
        def _():
            each(CHUNKS, finish)

    each(2 * CHUNKS - 1, step)

    def drain(c):
        cross(c).wait_send()
        turn(c).wait_send()
        for k in range(1, places):
            spread(c, k).wait_send()
        for k in range(1, ranks):
            swap(c, k).wait_send()

        @pl.when(ctx > 0)
        def _():
            rim(c).wait_send()

    each(CHUNKS, drain)

    @pl.when(jnp.logical_not(last))
    def _():
        each(CHUNKS, lambda c: lend(c).wait_send(), middle)

    each(places, lambda k: tap_z(k).wait_send(), 1)

    def drain_taps(p):
        tap_y(p).wait_send()
        tap_c(p, 0).wait_send()
        tap_c(p, 1).wait_send()

    each(places, drain_taps)


def shards(conv_input, gate_value, out_grad, filter_taps):
    _, rows, channels = conv_input.shape
    count = filter_taps.shape[0]
    members, ranks = lax.axis_size("dp"), lax.axis_size("ctx")
    taps = count * members
    wide = channels // CHUNKS
    if count % 8 or taps != rows or rows % 16 or members % 4 or channels % (128 * CHUNKS):
        return general(conv_input, gate_value, out_grad, filter_taps)
    pairs = members // 2
    places = pairs // 2
    scale = 1.0 / math.sqrt(rows * ranks * members)
    forward, inverse = transforms(rows + taps)
    hbm = pl.BlockSpec(memory_space=pl.ANY)
    bf, f32, dma, vmem = jnp.bfloat16, jnp.float32, pltpu.SemaphoreType.DMA, pltpu.VMEM
    out, fgrad = pl.pallas_call(
        functools.partial(kernel, pairs, ranks, scale),
        out_shape=(
            jax.ShapeDtypeStruct((rows, channels), bf),
            jax.ShapeDtypeStruct((count, channels), f32),
        ),
        in_specs=[hbm] * 6,
        out_specs=(pl.BlockSpec(memory_space=vmem),) * 2,
        scratch_shapes=[
            vmem((rows, channels), bf),
            vmem((rows, channels), bf),
            vmem((2 * rows, channels), bf),
            vmem((2 * rows, channels), bf),
            vmem((members, count, channels), bf),
            vmem((2, rows + taps, rows + taps), bf),
            vmem((2, rows + taps, rows + taps), bf),
            vmem((places, 2, 2, count, wide), f32),
            vmem((pairs, count, channels), f32),
            vmem((pairs, count, channels), bf),
            vmem((pairs, count, channels), bf),
            vmem((places, count, channels), f32),
            vmem((places, count, channels), bf),
            vmem((places, count, channels), bf),
            vmem((places, count, channels), bf),
            vmem((places, count, channels), bf),
            vmem((ranks, count, channels), bf),
            dma((CHUNKS,)), dma((CHUNKS,)), dma((CHUNKS,)), dma, dma((2,)),
            dma((CHUNKS,)), dma((CHUNKS,)), dma((CHUNKS,)), dma((CHUNKS,)),
            dma((places,)), dma((places,)), dma((places, 2)), dma((members,)),
            dma((CHUNKS,)), dma((CHUNKS,)), dma((CHUNKS,)), dma((CHUNKS,)),
            dma((places, CHUNKS)), dma((places, CHUNKS)),
            dma((ranks, CHUNKS)), dma((ranks, CHUNKS)),
        ],
        compiler_params=pltpu.CompilerParams(
            collective_id=0, has_side_effects=True, vmem_limit_bytes=65_900_000
        ),
    )(conv_input[0], gate_value[0], out_grad[0], filter_taps, jnp.asarray(np.stack(forward)), jnp.asarray(np.stack(inverse)))
    return out[None], fgrad


def solution(mesh):
    in_specs = (P("dp", "ctx", None), P("dp", "ctx", None), P("dp", "ctx", None), P("dp", None))
    out_specs = (P("dp", "ctx", None), P("dp", None))
    return jax.shard_map(shards, mesh=mesh, in_specs=in_specs, out_specs=out_specs, check_vma=False)
```

profile of v0, /device:TPU:0, one launch (start us, length us, event | category | flops | bytes accessed | tf_op | source)
XLA Modules:
  0.0 38.2 jit_solution(11270253703177606620)
XLA Ops:
  0.6 34.6 %shard_map.77 = (bf16[128,4096]{1,0:T(8,128)(2,1)}, f32[8,4096]{1,0:T(8,128)}) custom-call(bf16[128,4096]{1,0:T(8,128)(2,1)} %bitcast.4, bf16[128,4096]{1,0:T(8,128)(2,1)} %bitcast.5, bf16[128,4096]{1,0:T(8,128)(2,1)} %bitcast.6, bf16[8,4096]{1,0:T(8,128)(2,1)} %taps_hbm.1, bf16[2,256,256]{2,1,0:T(8,128)(2,1)} %constant.4.clone.f_hbm, ...), custom_call_target="tpu_custom_call" | custom-call | tf_op jit(solution)/shard_map/pallas_call | solution.py:402
  35.2 0.0 copy-start
  35.2 2.3 %copy.10 = bf16[1,128,4096]{2,1,0:T(8,128)(2,1)} copy(bf16[1,128,4096]{2,1,0:T(8,128)(2,1)} %bitcast.7) | data formatting | bytes 2097152
  37.5 0.0 copy-done
  37.5 0.7 %copy.11 = f32[8,4096]{1,0:T(8,128)} copy(f32[8,4096]{1,0:T(8,128)S(1)} %copy-done) | data formatting | bytes 262144
Async XLA Ops:
  35.2 2.3 %copy-start = (f32[8,4096]{1,0:T(8,128)S(1)}, f32[8,4096]{1,0:T(8,128)}, u32[]{:S(2)}) copy-start(f32[8,4096]{1,0:T(8,128)} %get-tuple-element.9) | copy-start | bytes 393220
where the time goes:
time: 38.3 us; the launch traced here: 38.2 us
  Pallas kernels  34.6 us (90%)
  local copies, waits for them, and re-layouts  2.98 us (8%)
  between operations  0.65 us (2%)
    pallas_call x1, Pallas kernels, shards(): pl.pallas_call(functools.partial(kernel, pairs, ranks, scale), out_shape=...  34.6 us
    unnamed x4, local copies, waits for them, and re-layouts  2.98 us

commit v1 on v0

--- a/solution.py
+++ b/solution.py
@@ -397,13 +397,13 @@
     places = pairs // 2
     scale = 1.0 / math.sqrt(rows * ranks * members)
     forward, inverse = transforms(rows + taps)
-    hbm = pl.BlockSpec(memory_space=pl.ANY)
+    hbm = pl.BlockSpec(memory_space=pltpu.HBM)
     bf, f32, dma, vmem = jnp.bfloat16, jnp.float32, pltpu.SemaphoreType.DMA, pltpu.VMEM
     out, fgrad = pl.pallas_call(
         functools.partial(kernel, pairs, ranks, scale),
         out_shape=(
-            jax.ShapeDtypeStruct((rows, channels), bf),
-            jax.ShapeDtypeStruct((count, channels), f32),
+            vmem((rows, channels), bf),
+            vmem((count, channels), f32),
         ),
         in_specs=[hbm] * 6,
         out_specs=(pl.BlockSpec(memory_space=vmem),) * 2,
@@ -433,10 +433,44 @@
             dma((ranks, CHUNKS)), dma((ranks, CHUNKS)),
         ],
         compiler_params=pltpu.CompilerParams(
-            collective_id=0, has_side_effects=True, vmem_limit_bytes=65_900_000
+            collective_id=0, has_side_effects=True, vmem_limit_bytes=40_000_000
         ),
-    )(conv_input[0], gate_value[0], out_grad[0], filter_taps, jnp.asarray(np.stack(forward)), jnp.asarray(np.stack(inverse)))
-    return out[None], fgrad
+    )(*(
+        pltpu.with_memory_space_constraint(x, pltpu.HBM)
+        for x in (conv_input[0], gate_value[0], out_grad[0], filter_taps, jnp.asarray(np.stack(forward)), jnp.asarray(np.stack(inverse)))
+    ))
+    return store(out, fgrad)
+
+
+PARTS = 8
+
+
+def store(grad, fgrad):
+    rows, channels = grad.shape
+    wide = channels // PARTS
+
+    def body(g_ref, f_ref, g_out, f_out, sems):
+        def copies():
+            for k in range(PARTS):
+                at = pl.ds(k * (rows // PARTS), rows // PARTS)
+                yield pltpu.make_async_copy(g_ref.at[at], g_out.at[0, at], sems.at[k])
+            yield pltpu.make_async_copy(f_ref, f_out, sems.at[PARTS])
+
+        for copy in copies():
+            copy.start()
+        for copy in copies():
+            copy.wait()
+
+    return pl.pallas_call(
+        body,
+        out_shape=(
+            jax.ShapeDtypeStruct((1, rows, channels), grad.dtype),
+            jax.ShapeDtypeStruct(fgrad.shape, fgrad.dtype),
+        ),
+        in_specs=[pl.BlockSpec(memory_space=pltpu.VMEM)] * 2,
+        out_specs=(pl.BlockSpec(memory_space=pl.ANY),) * 2,
+        scratch_shapes=[pltpu.SemaphoreType.DMA((PARTS + 1,))],
+    )(pltpu.with_memory_space_constraint(grad, pltpu.VMEM), pltpu.with_memory_space_constraint(fgrad, pltpu.VMEM))
 
 
 def solution(mesh):

time: 38.3 us -> 35.4 us (0.924)
  local copies, waits for them, and re-layouts: 2.98 us -> 0 us
    unnamed x4 -> x0, local copies, waits for them, and re-layouts: 2.98 us -> none
    pallas_call x0 -> x1, Pallas kernels: none -> 1.08 us  [store(): pl.pallas_call(body, out_shape=(jax.ShapeDtypeStruct((1, rows, channels),...]
    pallas_call x1, Pallas kernels: 34.6 us -> 33.5 us  [shards(): pl.pallas_call(functools.partial(kernel, pairs, ranks, scale), out_shape=...]
where the time goes in v1:
time: 35.4 us; the launch traced here: 35.3 us
  Pallas kernels  34.6 us (98%)
  between operations  0.64 us (2%)
    pallas_call x1, Pallas kernels, shards(): pl.pallas_call(functools.partial(kernel, pairs, ranks, scale), out_shape=...  33.5 us
    pallas_call x1, Pallas kernels, store(): pl.pallas_call(body, out_shape=(jax.ShapeDtypeStruct((1, rows, channels),...  1.08 us

profile of v1, /device:TPU:0, one launch (start us, length us, event | category | flops | bytes accessed | tf_op | source)
XLA Modules:
  0.0 35.3 jit_solution(13963140443357204399)
XLA Ops:
  0.6 33.5 %shard_map.77 = (bf16[128,4096]{1,0:T(8,128)(2,1)S(1)}, f32[8,4096]{1,0:T(8,128)S(1)}) custom-call(bf16[128,4096]{1,0:T(8,128)(2,1)} %bitcast.3, bf16[128,4096]{1,0:T(8,128)(2,1)} %bitcast.4, bf16[128,4096]{1,0:T(8,128)(2,1)} %bitcast.5, bf16[8,4096]{1,0:T(8,128)(2,1)} %taps_hbm.1, bf16[2,256,256]{2,1,0:T(8,128)(2,1)} %constant.4.clone.f_hbm, ...), custom_call_target="tpu_custom_call" | custom-call | tf_op jit(solution)/shard_map/pallas_call | solution.py:402
  34.2 1.1 %shard_map.78 = (bf16[1,128,4096]{2,1,0:T(8,128)(2,1)}, f32[8,4096]{1,0:T(8,128)}) custom-call(bf16[128,4096]{1,0:T(8,128)(2,1)S(1)} %get-tuple-element.4.g_ref, f32[8,4096]{1,0:T(8,128)S(1)} %get-tuple-element.5.f_ref), custom_call_target="tpu_custom_call" | custom-call | tf_op jit(solution)/shard_map/pallas_call | solution.py:464

commit v2 on v1

v2 whole, which is shorter than its diff:
```python
import functools
import math

import jax
import jax.numpy as jnp
import numpy as np
from jax import lax
from jax.experimental import pallas as pl
from jax.experimental.pallas import tpu as pltpu
from jax.sharding import PartitionSpec as P


def split(values):
    high = values.astype(jnp.bfloat16)
    return high, (values - high.astype(np.float32)).astype(jnp.bfloat16)


def transforms(length):
    half = length // 2
    angle = np.pi * np.outer(2 * np.arange(half) + 1, np.arange(length)) / length
    forward = np.concatenate([np.cos(angle), -np.sin(angle)], 0)
    inverse = np.concatenate([np.cos(angle), -np.sin(angle)], 0).T / half
    return split(forward.astype(np.float32)), split(inverse.astype(np.float32))


def dot(a, b):
    return lax.dot_general(a, b, (((1,), (0,)), ((), ())), preferred_element_type=jnp.float32)


def general(conv_input, gate_value, out_grad, filter_taps):
    inputs = conv_input[0]
    rows = inputs.shape[0]
    taps = filter_taps.shape[0] * lax.axis_size("dp")
    (fh, fl), (bh, bl) = transforms(rows + taps)
    half = (rows + taps) // 2
    mixed = (out_grad[0].astype(jnp.float32) * gate_value[0].astype(jnp.float32)).astype(
        jnp.bfloat16
    )
    devices = lax.axis_size("ctx")
    rim = lax.ppermute(mixed[:taps], "ctx", [(i + 1, i) for i in range(devices - 1)])
    full_taps = lax.all_gather(filter_taps, "dp", axis=0, tiled=True)

    def spectrum(x, first=0):
        n = x.shape[0]
        s = dot(fh[:, first : first + n], x) + dot(fl[:, first : first + n], x)
        return s[:half], s[half:]

    def back(re, im, n):
        s = jnp.concatenate([re, im], 0)
        high = s.astype(jnp.bfloat16)
        low = (s - high.astype(jnp.float32)).astype(jnp.bfloat16)
        return dot(bh[:n], high) + dot(bl[:n], high) + dot(bh[:n], low)

    xr, xi = spectrum(inputs)
    gr0, gi0 = spectrum(mixed)
    gr1, gi1 = spectrum(rim, rows)
    gr, gi = gr0 + gr1, gi0 + gi1
    partial = back(xr * gr + xi * gi, xr * gi - xi * gr, taps)
    hr, hi = spectrum(full_taps)
    grad = back(hr * gr + hi * gi, hr * gi - hi * gr, rows)
    shard_grad = lax.psum(lax.psum_scatter(partial, "dp", scatter_dimension=0, tiled=True), "ctx")
    tokens_all = rows * devices * lax.axis_size("dp")
    return (grad.astype(jnp.bfloat16)[None], shard_grad * (1.0 / math.sqrt(tokens_all)))


CHUNKS = 8
MESH = pl.DeviceIdType.MESH


def kernel(
    pairs, scale,
    in_hbm, gate_hbm, cot_hbm, taps_hbm, f_hbm,
    obuf, fbuf,
    x_gc, x_in, g, inc, taps_all, f_all, xs, gs, hs, p32, own32, csrc, cbuf, half32, ysrc, ybuf,
    zsrc, zbuf, xbuf,
    ld_gc, ld_in, ld_taps, ld_f, met,
    inc_s, inc_r, tz_s, tz_r, ty_s, ty_r, tc_s, tc_r,
    c_s, c_r, y_s, y_r, z_s, z_r, x_s, x_r,
):
    dp, ctx = lax.axis_index("dp"), lax.axis_index("ctx")
    core, mine = lax.rem(dp, 2), dp // 2
    partner = dp + 1 - 2 * core
    side, place, places = lax.rem(mine, 2), mine // 2, pairs // 2
    across = 2 * (mine + 1 - 2 * side) + core
    rows, channels = g.shape
    wide = channels // CHUNKS
    middle = CHUNKS // 2
    first, last = ctx == 0, ctx == 1
    other = 1 - ctx
    f32, bf = jnp.float32, jnp.bfloat16
    count = taps_all.shape[1]
    half = rows

    def cols(c):
        return pl.ds(pl.multiple_of(c * wide, wide), wide)

    def each(n, body, start=0):
        lax.fori_loop(start, n, lambda i, z: (body(i), z)[1], 0)

    def local(src, dst, sem):
        return pltpu.make_async_copy(src, dst, sem)

    def remote(src, dst, send, recv, to):
        return pltpu.make_async_remote_copy(
            src_ref=src, dst_ref=dst, send_sem=send, recv_sem=recv, device_id=to, device_id_type=MESH
        )

    own_taps = local(taps_hbm, taps_all.at[dp], ld_taps)
    load_f = local(f_hbm, f_all, ld_f)
    load_in = local(in_hbm, x_in, ld_in)

    def loads(c):
        local(cot_hbm.at[:, cols(c)], x_gc.at[0, :, cols(c)], ld_gc.at[c]).start()
        local(gate_hbm.at[:, cols(c)], x_gc.at[1, :, cols(c)], ld_gc.at[c]).start()

    each(CHUNKS, loads)

    barrier = pltpu.get_barrier_semaphore()

    @pl.when(first)
    def _():
        pl.semaphore_signal(barrier, inc=1, device_id=(dp, other), device_id_type=MESH)

    own_taps.start()
    load_f.start()
    load_in.start()

    @pl.when(last)
    def _():
        pl.semaphore_wait(barrier, 1)
        pl.semaphore_signal(met, inc=1, device_id=(dp, other), device_id_type=MESH)

    def z_peer(k):
        return lax.rem(place + k, places)

    def z_device(k):
        return 4 * z_peer(k) + 2 * side + core

    def rim(c):
        return remote(g.at[:, cols(c)], inc.at[:, cols(c)], inc_s, inc_r.at[c], (dp, other))

    def lend(c):
        return remote(in_hbm.at[:, cols(c)], inc.at[:, cols(c)], inc_s, inc_r.at[c], (dp, other))

    def mix(c):
        both = x_gc.at[:, :, cols(c)]
        local(both, both, ld_gc.at[c]).wait()
        a = x_gc[0, :, cols(c)].astype(f32)
        b = x_gc[1, :, cols(c)].astype(f32)
        g[:, cols(c)] = (a * b).astype(bf)

        @pl.when(last)
        def _():
            rim(c).start()

    each(CHUNKS, mix)

    @pl.when(first)
    def _():
        pl.semaphore_wait(met, 1)
        pl.semaphore_signal(barrier, inc=1, device_id=(partner, ctx), device_id_type=MESH)
        pl.semaphore_signal(barrier, inc=1, device_id=(across, ctx), device_id_type=MESH)
        for k in range(1, places):
            pl.semaphore_signal(barrier, inc=1, device_id=(z_device(k), ctx), device_id_type=MESH)
        each(CHUNKS, lambda c: lend(c).start(), middle)

    def ahead(which, x):
        return jnp.dot(f_all[which], jnp.concatenate([x, x], 0), preferred_element_type=f32)

    def correlate(a, b):
        ar, ai, br, bi = a[:half], a[half:], b[:half], b[half:]
        value = jnp.concatenate([ar * br + ai * bi, ar * bi - ai * br], 0)
        high = value.astype(bf)
        low = (value - high.astype(f32)).astype(bf)
        both = jnp.dot(f_all[2], high, preferred_element_type=f32)
        return both[:half] + both[half:] + jnp.dot(f_all[2, :half, :], low, preferred_element_type=f32)

    def chunk(i):
        return jnp.where(last, i, lax.rem(i + middle, CHUNKS))

    def emit(a, b, c):
        p32[...] = correlate(a, b).reshape(places, 2, 2, count, wide)
        for s in range(2):
            csrc[pl.ds(s * places, places), :, cols(c)] = p32[:, s, 1 - core].astype(bf)
            own32[pl.ds(s * places, places), :, cols(c)] = p32[:, s, core]

    def front(i):
        c = chunk(i)
        a, b = ahead(0, x_in[:, cols(c)]), ahead(0, g[:, cols(c)])
        gs[:, cols(c)] = b

        @pl.when(i < middle)
        def _():
            emit(a, b, c)

        @pl.when(i >= middle)
        def _():
            xs[:, cols(c)] = a

    load_f.wait()
    load_in.wait()
    each(CHUNKS, front)

    @pl.when(first)
    def _():
        pl.semaphore_wait(barrier, places + 1)
        pl.semaphore_signal(met, inc=1, device_id=(dp, other), device_id_type=MESH)

    @pl.when(last)
    def _():
        pl.semaphore_wait(met, 1)

    def shard(p, s, c):
        return taps_all.at[4 * p + 2 * s + c]

    def tap_z(k):
        return remote(shard(place, side, core), shard(place, side, core), tz_s, tz_r.at[place], (z_device(k), ctx))

    def tap_y(p):
        return remote(shard(p, side, core), shard(p, side, core), ty_s, ty_r.at[p], (across, ctx))

    def tap_c(p, s):
        return remote(shard(p, s, core), shard(p, s, core), tc_s, tc_r, (partner, ctx))

    def tap_wait(p, s, sem):
        remote(shard(p, s, core), shard(p, s, core), tz_s, sem, (partner, ctx)).wait_recv()

    def pass_y(k):
        p = z_peer(k)
        tap_wait(p, side, tz_r.at[p])
        tap_y(p).start()
        tap_c(p, side).start()

    def pass_c(p):
        tap_wait(p, 1 - side, ty_r.at[p])
        tap_c(p, 1 - side).start()

    def cross(c):
        return remote(csrc.at[:, :, cols(c)], cbuf.at[:, :, cols(c)], c_s, c_r.at[c], (partner, ctx))

    def turn(c):
        return remote(ysrc.at[:, :, cols(c)], ybuf.at[:, :, cols(c)], y_s, y_r.at[c], (across, ctx))

    def spread(c, k):
        return remote(
            zsrc.at[z_peer(k), :, cols(c)], zbuf.at[place, :, cols(c)], z_s, z_r.at[c], (z_device(k), ctx)
        )

    def gathered(c):
        slots = zbuf.at[pl.ds(0, places - 1), :, cols(c)]
        return remote(slots, slots, z_s, z_r.at[c], (z_device(1), ctx))

    def swap(c):
        slot = xbuf.at[ctx, :, cols(c)]
        return remote(slot, slot, x_s, x_r, (dp, other))

    def stage2(i):
        c = chunk(i)
        cross(c).wait_recv()
        there, here = pl.ds((1 - side) * places, places), pl.ds(side * places, places)
        ysrc[:, :, cols(c)] = (own32[there, :, cols(c)] + cbuf[there, :, cols(c)].astype(f32)).astype(bf)
        turn(c).start()
        half32[:, :, cols(c)] = own32[here, :, cols(c)] + cbuf[here, :, cols(c)].astype(f32)

    def stage3(i):
        c = chunk(i)
        turn(c).wait_recv()
        total = half32[:, :, cols(c)] + ybuf[:, :, cols(c)].astype(f32)
        half32[:, :, cols(c)] = total
        zsrc[:, :, cols(c)] = total.astype(bf)
        for k in range(1, places):
            spread(c, k).start()

    def stage4(i):
        c = chunk(i)
        gathered(c).wait_recv()
        total = half32[place, :, cols(c)]
        for k in range(1, places):
            total = total + zbuf[z_peer(k), :, cols(c)].astype(f32)
        xbuf[ctx, :, cols(c)] = total.astype(bf)
        swap(c).start()

    keep, drop = other.astype(f32), ctx.astype(f32)

    def arrive(c):
        remote(inc.at[:, cols(c)], inc.at[:, cols(c)], inc_s, inc_r.at[c], (dp, other)).wait_recv()
        return ahead(1, inc[:, cols(c)])

    def meet(i):
        c = chunk(i)
        w = arrive(c)
        b = gs[:, cols(c)] + keep * w
        gs[:, cols(c)] = b
        emit(xs[:, cols(c)] - drop * w, b, c)
        cross(c).start()

    def spectrum(c):
        t = taps_all[:, :, cols(c)].astype(f32).reshape(rows, wide).astype(bf)
        hs[:, cols(c)] = ahead(0, t)

    def grad(c):
        @pl.when(jnp.logical_and(first, c >= middle))
        def _():
            gs[:, cols(c)] += arrive(c)

        obuf[:, cols(c)] = correlate(hs[:, cols(c)], gs[:, cols(c)]).astype(bf)

    own_taps.wait()
    each(places, lambda k: tap_z(k).start(), 1)
    tap_y(place).start()
    tap_c(place, side).start()
    each(middle, lambda i: cross(chunk(i)).start())

    def at(i, when, action):
        @pl.when(i == when)
        def _():
            action()

    def follow(i):
        meet(i)
        at(i, middle, lambda: each(middle, stage2))
        at(i, middle + 1, lambda: each(middle, stage3))
        at(i, middle + 1, lambda: pass_y(1))

        @pl.when(i > middle)
        def _():
            stage2(i - 1)

        @pl.when(i > middle + 1)
        def _():
            stage3(i - 2)

        at(i, middle + 2, lambda: each(places, pass_y, 2))
        at(i, middle + 3, lambda: each(middle, stage4))

    each(CHUNKS, follow, middle)

    each(places, pass_c)
    theirs = taps_all.at[pl.ds(0, pairs)]
    remote(theirs, theirs, tc_s, tc_r, (partner, ctx)).wait_recv()
    each(CHUNKS, spectrum)

    def slot(c):
        grad(c)
        at(c, 1, lambda: stage2(CHUNKS - 1))
        at(c, 2, lambda: stage3(CHUNKS - 2))
        at(c, 3, lambda: stage4(middle))
        at(c, 4, lambda: stage3(CHUNKS - 1))
        at(c, 5, lambda: each(CHUNKS - 1, stage4, middle + 1))
        at(c, 6, lambda: stage4(CHUNKS - 1))

    each(CHUNKS, slot)

    theirs = xbuf.at[other]
    remote(theirs, theirs, x_s, x_r, (dp, other)).wait_recv()
    fbuf[...] = (xbuf[0].astype(f32) + xbuf[1].astype(f32)) * scale

    def sent(ref, sem):
        remote(ref, ref, sem, x_r, (dp, other)).wait_send()

    sent(csrc, c_s)
    sent(ysrc, y_s)
    sent(zsrc.at[pl.ds(0, places - 1)], z_s)
    sent(xbuf.at[ctx], x_s)
    sent(taps_all.at[pl.ds(0, places - 1)], tz_s)
    sent(taps_all.at[pl.ds(0, places)], ty_s)
    sent(taps_all.at[pl.ds(0, pairs)], tc_s)

    @pl.when(last)
    def _():
        sent(g, inc_s)

    @pl.when(first)
    def _():
        sent(g.at[:, pl.ds(0, channels // 2)], inc_s)


def shards(conv_input, gate_value, out_grad, filter_taps):
    _, rows, channels = conv_input.shape
    count = filter_taps.shape[0]
    members, ranks = lax.axis_size("dp"), lax.axis_size("ctx")
    taps = count * members
    wide = channels // CHUNKS
    if ranks != 2 or count % 8 or taps != rows or rows % 16 or members % 4 or channels % (128 * CHUNKS):
        return general(conv_input, gate_value, out_grad, filter_taps)
    pairs = members // 2
    places = pairs // 2
    scale = 1.0 / math.sqrt(rows * ranks * members)
    (fh, fl), (bh, bl) = transforms(rows + taps)
    matrices = np.stack([
        np.concatenate([fh[:, :rows], fl[:, :rows]], 1),
        np.concatenate([fh[:, rows:], fl[:, rows:]], 1),
        np.concatenate([bh[:rows], bl[:rows]], 0),
    ])
    hbm = pl.BlockSpec(memory_space=pltpu.HBM)
    bf, f32, dma, vmem = jnp.bfloat16, jnp.float32, pltpu.SemaphoreType.DMA, pltpu.VMEM
    out, fgrad = pl.pallas_call(
        functools.partial(kernel, pairs, scale),
        out_shape=(vmem((rows, channels), bf), vmem((count, channels), f32)),
        in_specs=[hbm] * 5,
        out_specs=(pl.BlockSpec(memory_space=vmem),) * 2,
        scratch_shapes=[
            vmem((2, rows, channels), bf),
            vmem((rows, channels), bf),
            vmem((rows, channels), bf),
            vmem((rows, channels), bf),
            vmem((members, count, channels), bf),
            vmem((3, rows + taps, rows + taps), bf),
            vmem((rows + taps, channels), f32),
            vmem((rows + taps, channels), f32),
            vmem((rows + taps, channels), f32),
            vmem((places, 2, 2, count, wide), f32),
            vmem((pairs, count, channels), f32),
            vmem((pairs, count, channels), bf),
            vmem((pairs, count, channels), bf),
            vmem((places, count, channels), f32),
            vmem((places, count, channels), bf),
            vmem((places, count, channels), bf),
            vmem((places, count, channels), bf),
            vmem((places, count, channels), bf),
            vmem((ranks, count, channels), bf),
            dma((CHUNKS,)), dma, dma, dma, pltpu.SemaphoreType.REGULAR,
            dma, dma((CHUNKS,)), dma, dma((places,)), dma, dma((places,)), dma, dma,
            dma, dma((CHUNKS,)), dma, dma((CHUNKS,)), dma, dma((CHUNKS,)), dma, dma,
        ],
        compiler_params=pltpu.CompilerParams(
            collective_id=0, has_side_effects=True, vmem_limit_bytes=48_000_000
        ),
    )(*(
        pltpu.with_memory_space_constraint(x, pltpu.HBM)
        for x in (conv_input[0], gate_value[0], out_grad[0], filter_taps, jnp.asarray(matrices))
    ))
    return store(out, fgrad)


PARTS = 8


def store(grad, fgrad):
    rows, channels = grad.shape
    wide = channels // PARTS

    def body(g_ref, f_ref, g_out, f_out, sems):
        def copies():
            for k in range(PARTS):
                at = pl.ds(k * (rows // PARTS), rows // PARTS)
                yield pltpu.make_async_copy(g_ref.at[at], g_out.at[0, at], sems.at[k])
            yield pltpu.make_async_copy(f_ref, f_out, sems.at[PARTS])

        for copy in copies():
            copy.start()
        for copy in copies():
            copy.wait()

    return pl.pallas_call(
        body,
        out_shape=(
            jax.ShapeDtypeStruct((1, rows, channels), grad.dtype),
            jax.ShapeDtypeStruct(fgrad.shape, fgrad.dtype),
        ),
        in_specs=[pl.BlockSpec(memory_space=pltpu.VMEM)] * 2,
        out_specs=(pl.BlockSpec(memory_space=pl.ANY),) * 2,
        scratch_shapes=[pltpu.SemaphoreType.DMA((PARTS + 1,))],
    )(pltpu.with_memory_space_constraint(grad, pltpu.VMEM), pltpu.with_memory_space_constraint(fgrad, pltpu.VMEM))


def solution(mesh):
    in_specs = (P("dp", "ctx", None), P("dp", "ctx", None), P("dp", "ctx", None), P("dp", None))
    out_specs = (P("dp", "ctx", None), P("dp", None))
    return jax.shard_map(shards, mesh=mesh, in_specs=in_specs, out_specs=out_specs, check_vma=False)
```

time: 35.4 us -> 40.5 us (1.14)
  Pallas kernels: 34.6 us -> 39.7 us
    pallas_call x1, Pallas kernels: 33.5 us -> 38.6 us  [shards(): pl.pallas_call(functools.partial(kernel, pairs, scale), out_shape=(vmem((...]
where the time goes in v2:
time: 40.5 us; the launch traced here: 40.4 us
  Pallas kernels  39.7 us (98%)
  between operations  0.64 us (2%)
    pallas_call x1, Pallas kernels, shards(): pl.pallas_call(functools.partial(kernel, pairs, scale), out_shape=(vmem((...  38.6 us
    pallas_call x1, Pallas kernels, store(): pl.pallas_call(body, out_shape=(jax.ShapeDtypeStruct((1, rows, channels),...  1.08 us

profile of v2, /device:TPU:0, one launch (start us, length us, event | category | flops | bytes accessed | tf_op | source)
XLA Modules:
  0.0 40.4 jit_solution(10896636540132407736)
XLA Ops:
  0.6 38.6 %shard_map.68 = (bf16[128,4096]{1,0:T(8,128)(2,1)S(1)}, f32[8,4096]{1,0:T(8,128)S(1)}) custom-call(bf16[128,4096]{1,0:T(8,128)(2,1)} %bitcast.3, bf16[128,4096]{1,0:T(8,128)(2,1)} %bitcast.4, bf16[128,4096]{1,0:T(8,128)(2,1)} %bitcast.5, bf16[8,4096]{1,0:T(8,128)(2,1)} %taps_hbm.1, bf16[3,256,256]{2,1,0:T(8,128)(2,1)} %constant.2.clone.f_hbm), custom_call_target="tpu_custom_call" | custom-call | tf_op jit(solution)/shard_map/pallas_call | solution.py:397
  39.3 1.1 %shard_map.69 = (bf16[1,128,4096]{2,1,0:T(8,128)(2,1)}, f32[8,4096]{1,0:T(8,128)}) custom-call(bf16[128,4096]{1,0:T(8,128)(2,1)S(1)} %get-tuple-element.4.g_ref, f32[8,4096]{1,0:T(8,128)S(1)} %get-tuple-element.5.f_ref), custom_call_target="tpu_custom_call" | custom-call | tf_op jit(solution)/shard_map/pallas_call | solution.py:455

commit v3 on v2

--- a/solution.py
+++ b/solution.py
@@ -64,6 +64,8 @@
 
 
 CHUNKS = 8
+EARLY = 2
+LATE = 4
 MESH = pl.DeviceIdType.MESH
 
 
@@ -197,19 +199,6 @@
         def _():
             xs[:, cols(c)] = a
 
-    load_f.wait()
-    load_in.wait()
-    each(CHUNKS, front)
-
-    @pl.when(first)
-    def _():
-        pl.semaphore_wait(barrier, places + 1)
-        pl.semaphore_signal(met, inc=1, device_id=(dp, other), device_id_type=MESH)
-
-    @pl.when(last)
-    def _():
-        pl.semaphore_wait(met, 1)
-
     def shard(p, s, c):
         return taps_all.at[4 * p + 2 * s + c]
 
@@ -305,49 +294,68 @@
 
         obuf[:, cols(c)] = correlate(hs[:, cols(c)], gs[:, cols(c)]).astype(bf)
 
-    own_taps.wait()
-    each(places, lambda k: tap_z(k).start(), 1)
-    tap_y(place).start()
-    tap_c(place, side).start()
-    each(middle, lambda i: cross(chunk(i)).start())
-
-    def at(i, when, action):
+    def at(i, when, *actions):
         @pl.when(i == when)
         def _():
-            action()
+            for action in actions:
+                action()
+
+    def meet_plane():
+        @pl.when(first)
+        def _():
+            pl.semaphore_wait(barrier, places + 1)
+            pl.semaphore_signal(met, inc=1, device_id=(dp, other), device_id_type=MESH)
+
+        @pl.when(last)
+        def _():
+            pl.semaphore_wait(met, 1)
+
+        own_taps.wait()
+        each(places, lambda k: tap_z(k).start(), 1)
+        tap_y(place).start()
+        tap_c(place, side).start()
+        each(EARLY, lambda i: cross(chunk(i)).start())
+
+    def begin(i):
+        front(i)
+
+        @pl.when(jnp.logical_and(i >= EARLY, i < middle))
+        def _():
+            cross(chunk(i)).start()
+
+        at(i, EARLY - 1, meet_plane)
+
+    load_f.wait()
+    load_in.wait()
+    each(CHUNKS, begin)
+    each(middle, stage2)
 
     def follow(i):
         meet(i)
-        at(i, middle, lambda: each(middle, stage2))
+        at(i, middle, lambda: pass_y(1))
         at(i, middle + 1, lambda: each(middle, stage3))
-        at(i, middle + 1, lambda: pass_y(1))
-
-        @pl.when(i > middle)
-        def _():
-            stage2(i - 1)
-
-        @pl.when(i > middle + 1)
-        def _():
-            stage3(i - 2)
-
-        at(i, middle + 2, lambda: each(places, pass_y, 2))
-        at(i, middle + 3, lambda: each(middle, stage4))
+        stage2(i)
+        at(i, middle + 1, lambda: each(places, pass_y, 2), lambda: stage3(middle))
+        at(i, middle + 2, lambda: each(middle, stage4), lambda: stage3(middle + 1))
 
     each(CHUNKS, follow, middle)
 
     each(places, pass_c)
+    stage4(middle)
+    stage3(middle + 2)
     theirs = taps_all.at[pl.ds(0, pairs)]
     remote(theirs, theirs, tc_s, tc_r, (partner, ctx)).wait_recv()
-    each(CHUNKS, spectrum)
+
+    def spectra(c):
+        spectrum(c)
+        at(c, middle - 1, lambda: stage4(middle + 1), lambda: stage3(middle + 3))
+
+    each(CHUNKS, spectra)
 
     def slot(c):
         grad(c)
-        at(c, 1, lambda: stage2(CHUNKS - 1))
-        at(c, 2, lambda: stage3(CHUNKS - 2))
-        at(c, 3, lambda: stage4(middle))
-        at(c, 4, lambda: stage3(CHUNKS - 1))
-        at(c, 5, lambda: each(CHUNKS - 1, stage4, middle + 1))
-        at(c, 6, lambda: stage4(CHUNKS - 1))
+        at(c, 0, lambda: stage4(middle + 2))
+        at(c, LATE, lambda: stage4(middle + 3))
 
     each(CHUNKS, slot)
 

time: 40.5 us -> 32.8 us (0.81)
  Pallas kernels: 39.7 us -> 32 us
    pallas_call x1, Pallas kernels: 38.6 us -> 31 us  [shards(): pl.pallas_call(functools.partial(kernel, pairs, scale), out_shape=(vmem((...]
where the time goes in v3:
time: 32.8 us; the launch traced here: 32.7 us
  Pallas kernels  32 us (98%)
  between operations  0.64 us (2%)
    pallas_call x1, Pallas kernels, shards(): pl.pallas_call(functools.partial(kernel, pairs, scale), out_shape=(vmem((...  31 us
    pallas_call x1, Pallas kernels, store(): pl.pallas_call(body, out_shape=(jax.ShapeDtypeStruct((1, rows, channels),...  1.08 us

profile of v3, /device:TPU:0, one launch (start us, length us, event | category | flops | bytes accessed | tf_op | source)
XLA Modules:
  0.0 32.7 jit_solution(16540611546731653546)
XLA Ops:
  0.6 31.0 %shard_map.68 = (bf16[128,4096]{1,0:T(8,128)(2,1)S(1)}, f32[8,4096]{1,0:T(8,128)S(1)}) custom-call(bf16[128,4096]{1,0:T(8,128)(2,1)} %bitcast.3, bf16[128,4096]{1,0:T(8,128)(2,1)} %bitcast.4, bf16[128,4096]{1,0:T(8,128)(2,1)} %bitcast.5, bf16[8,4096]{1,0:T(8,128)(2,1)} %taps_hbm.1, bf16[3,256,256]{2,1,0:T(8,128)(2,1)} %constant.2.clone.f_hbm), custom_call_target="tpu_custom_call" | custom-call | tf_op jit(solution)/shard_map/pallas_call | solution.py:405
  31.6 1.1 %shard_map.69 = (bf16[1,128,4096]{2,1,0:T(8,128)(2,1)}, f32[8,4096]{1,0:T(8,128)}) custom-call(bf16[128,4096]{1,0:T(8,128)(2,1)S(1)} %get-tuple-element.4.g_ref, f32[8,4096]{1,0:T(8,128)S(1)} %get-tuple-element.5.f_ref), custom_call_target="tpu_custom_call" | custom-call | tf_op jit(solution)/shard_map/pallas_call | solution.py:463

commit v4 on v3

--- a/solution.py
+++ b/solution.py
@@ -65,7 +65,7 @@
 
 CHUNKS = 8
 EARLY = 2
-LATE = 4
+LATE = 3
 MESH = pl.DeviceIdType.MESH
 
 
@@ -151,7 +151,7 @@
         b = x_gc[1, :, cols(c)].astype(f32)
         g[:, cols(c)] = (a * b).astype(bf)
 
-        @pl.when(last)
+        @pl.when(jnp.logical_and(last, jnp.logical_or(core == 0, c < middle)))
         def _():
             rim(c).start()
 
@@ -333,29 +333,41 @@
     def follow(i):
         meet(i)
         at(i, middle, lambda: pass_y(1))
-        at(i, middle + 1, lambda: each(middle, stage3))
-        stage2(i)
-        at(i, middle + 1, lambda: each(places, pass_y, 2), lambda: stage3(middle))
-        at(i, middle + 2, lambda: each(middle, stage4), lambda: stage3(middle + 1))
+        at(i, middle + 1, lambda: each(places, pass_y, 2))
+        at(i, middle + 2, lambda: each(middle, stage3))
+
+        @pl.when(jnp.logical_and(i == middle + 1, jnp.logical_and(last, core == 1)))
+        def _():
+            each(CHUNKS, lambda c: rim(c).start(), middle)
+
+        @pl.when(i < CHUNKS - 1)
+        def _():
+            stage2(i)
 
     each(CHUNKS, follow, middle)
 
+    stage2(CHUNKS - 1)
+    stage3(middle)
+    stage3(middle + 1)
     each(places, pass_c)
-    stage4(middle)
     stage3(middle + 2)
     theirs = taps_all.at[pl.ds(0, pairs)]
     remote(theirs, theirs, tc_s, tc_r, (partner, ctx)).wait_recv()
 
     def spectra(c):
         spectrum(c)
-        at(c, middle - 1, lambda: stage4(middle + 1), lambda: stage3(middle + 3))
+        at(c, 3, lambda: stage3(CHUNKS - 1))
 
     each(CHUNKS, spectra)
+    each(middle + 2, stage4)
 
     def slot(c):
         grad(c)
         at(c, 0, lambda: stage4(middle + 2))
-        at(c, LATE, lambda: stage4(middle + 3))
+
+        @pl.when(c == jnp.where(last, 1, LATE))
+        def _():
+            stage4(CHUNKS - 1)
 
     each(CHUNKS, slot)
 

time: 32.8 us -> 31.9 us (0.973)
  Pallas kernels: 32 us -> 31.1 us
    pallas_call x1, Pallas kernels: 31 us -> 30 us  [shards(): pl.pallas_call(functools.partial(kernel, pairs, scale), out_shape=(vmem((...]
where the time goes in v4:
time: 31.9 us; the launch traced here: 31.7 us
  Pallas kernels  31.1 us (97%)
  between operations  0.64 us (2%)
    pallas_call x1, Pallas kernels, shards(): pl.pallas_call(functools.partial(kernel, pairs, scale), out_shape=(vmem((...  30 us
    pallas_call x1, Pallas kernels, store(): pl.pallas_call(body, out_shape=(jax.ShapeDtypeStruct((1, rows, channels),...  1.08 us

profile of v4, /device:TPU:0, one launch (start us, length us, event | category | flops | bytes accessed | tf_op | source)
XLA Modules:
  0.0 31.7 jit_solution(5872345415301815803)
XLA Ops:
  0.6 30.0 %shard_map.68 = (bf16[128,4096]{1,0:T(8,128)(2,1)S(1)}, f32[8,4096]{1,0:T(8,128)S(1)}) custom-call(bf16[128,4096]{1,0:T(8,128)(2,1)} %bitcast.3, bf16[128,4096]{1,0:T(8,128)(2,1)} %bitcast.4, bf16[128,4096]{1,0:T(8,128)(2,1)} %bitcast.5, bf16[8,4096]{1,0:T(8,128)(2,1)} %taps_hbm.1, bf16[3,256,256]{2,1,0:T(8,128)(2,1)} %constant.2.clone.f_hbm), custom_call_target="tpu_custom_call" | custom-call | tf_op jit(solution)/shard_map/pallas_call | solution.py:417
  30.7 1.1 %shard_map.69 = (bf16[1,128,4096]{2,1,0:T(8,128)(2,1)}, f32[8,4096]{1,0:T(8,128)}) custom-call(bf16[128,4096]{1,0:T(8,128)(2,1)S(1)} %get-tuple-element.4.g_ref, f32[8,4096]{1,0:T(8,128)S(1)} %get-tuple-element.5.f_ref), custom_call_target="tpu_custom_call" | custom-call | tf_op jit(solution)/shard_map/pallas_call | solution.py:475

commit v5 on v4

--- a/solution.py
+++ b/solution.py
@@ -65,7 +65,6 @@
 
 CHUNKS = 8
 EARLY = 2
-LATE = 3
 MESH = pl.DeviceIdType.MESH
 
 
@@ -74,10 +73,10 @@
     in_hbm, gate_hbm, cot_hbm, taps_hbm, f_hbm,
     obuf, fbuf,
     x_gc, x_in, g, inc, taps_all, f_all, xs, gs, hs, p32, own32, csrc, cbuf, half32, ysrc, ybuf,
-    zsrc, zbuf, xbuf,
-    ld_gc, ld_in, ld_taps, ld_f, met,
+    zsrc, zbuf, xbuf, vbuf,
+    ld_gc, ld_in, ld_taps, ld_f, met, line,
     inc_s, inc_r, tz_s, tz_r, ty_s, ty_r, tc_s, tc_r,
-    c_s, c_r, y_s, y_r, z_s, z_r, x_s, x_r,
+    c_s, c_r, y_s, y_r, z_s, z_r, x_s, x_r, v_s, v_r,
 ):
     dp, ctx = lax.axis_index("dp"), lax.axis_index("ctx")
     core, mine = lax.rem(dp, 2), dp // 2
@@ -163,7 +162,9 @@
         pl.semaphore_signal(barrier, inc=1, device_id=(partner, ctx), device_id_type=MESH)
         pl.semaphore_signal(barrier, inc=1, device_id=(across, ctx), device_id_type=MESH)
         for k in range(1, places):
-            pl.semaphore_signal(barrier, inc=1, device_id=(z_device(k), ctx), device_id_type=MESH)
+            @pl.when(z_peer(k) > place)
+            def _(k=k):
+                pl.semaphore_signal(barrier, inc=1, device_id=(z_device(k), ctx), device_id_type=MESH)
         each(CHUNKS, lambda c: lend(c).start(), middle)
 
     def ahead(which, x):
@@ -214,8 +215,9 @@
     def tap_wait(p, s, sem):
         remote(shard(p, s, core), shard(p, s, core), tz_s, sem, (partner, ctx)).wait_recv()
 
-    def pass_y(k):
-        p = z_peer(k)
+    def pass_y(j):
+        inner = jnp.where(j == 1, places - 1, j - 1)
+        p = z_peer(jnp.where(place == 0, j, jnp.where(place == places - 1, places - j, inner)))
         tap_wait(p, side, tz_r.at[p])
         tap_y(p).start()
         tap_c(p, side).start()
@@ -269,6 +271,32 @@
         xbuf[ctx, :, cols(c)] = total.astype(bf)
         swap(c).start()
 
+    tail = chunk(CHUNKS - 1)
+    theirs_tail = jnp.where(last, middle - 1, CHUNKS - 1)
+    few = pl.ds(0, channels - wide)
+
+    def direct(k, to):
+        return remote(
+            zsrc.at[z_peer(k), :, cols(tail)], vbuf.at[ctx * places + place], v_s, v_r, (z_device(k), to)
+        )
+
+    def finish3():
+        turn(tail).wait_recv()
+        total = half32[:, :, cols(tail)] + ybuf[:, :, cols(tail)].astype(f32)
+        zsrc[:, :, cols(tail)] = total.astype(bf)
+        for k in range(1, places):
+            direct(k, other).start()
+        direct(0, other).start()
+        for k in range(1, places):
+            direct(k, ctx).start()
+        vbuf[ctx * places + place] = zsrc[place, :, cols(tail)]
+
+    def summed(r):
+        total = vbuf[r * places].astype(f32)
+        for p in range(1, places):
+            total = total + vbuf[r * places + p].astype(f32)
+        return total.astype(bf)
+
     keep, drop = other.astype(f32), ctx.astype(f32)
 
     def arrive(c):
@@ -303,19 +331,49 @@
     def meet_plane():
         @pl.when(first)
         def _():
-            pl.semaphore_wait(barrier, places + 1)
+            pl.semaphore_wait(barrier, 2 + place)
             pl.semaphore_signal(met, inc=1, device_id=(dp, other), device_id_type=MESH)
+            for k in range(1, places):
+                @pl.when(z_peer(k) < place)
+                def _(k=k):
+                    pl.semaphore_signal(line, inc=1, device_id=(z_device(k), ctx), device_id_type=MESH)
 
         @pl.when(last)
         def _():
             pl.semaphore_wait(met, 1)
 
         own_taps.wait()
-        each(places, lambda k: tap_z(k).start(), 1)
+
+        def lower(k):
+            @pl.when(z_peer(k) < place)
+            def _():
+                tap_z(k).start()
+
+        each(places, lower, 1)
         tap_y(place).start()
         tap_c(place, side).start()
         each(EARLY, lambda i: cross(chunk(i)).start())
 
+    def meet_line():
+        @pl.when(first)
+        def _():
+            @pl.when(place < places - 1)
+            def _():
+                pl.semaphore_wait(line, places - 1 - place)
+
+            pl.semaphore_signal(line, inc=1, device_id=(dp, other), device_id_type=MESH)
+
+        @pl.when(last)
+        def _():
+            pl.semaphore_wait(line, 1)
+
+        def upper(k):
+            @pl.when(z_peer(k) > place)
+            def _():
+                tap_z(k).start()
+
+        each(places, upper, 1)
+
     def begin(i):
         front(i)
 
@@ -324,11 +382,16 @@
             cross(chunk(i)).start()
 
         at(i, EARLY - 1, meet_plane)
+
+        @pl.when(i == jnp.where(place == places - 1, EARLY - 1, jnp.where(place == 0, CHUNKS - 1, CHUNKS - 3)))
+        def _():
+            meet_line()
+
+        at(i, CHUNKS - 3, lambda: each(middle, stage2))
 
     load_f.wait()
     load_in.wait()
     each(CHUNKS, begin)
-    each(middle, stage2)
 
     def follow(i):
         meet(i)
@@ -336,7 +399,7 @@
         at(i, middle + 1, lambda: each(places, pass_y, 2))
         at(i, middle + 2, lambda: each(middle, stage3))
 
-        @pl.when(jnp.logical_and(i == middle + 1, jnp.logical_and(last, core == 1)))
+        @pl.when(jnp.logical_and(i == CHUNKS - 1, jnp.logical_and(last, core == 1)))
         def _():
             each(CHUNKS, lambda c: rim(c).start(), middle)
 
@@ -356,23 +419,24 @@
 
     def spectra(c):
         spectrum(c)
-        at(c, 3, lambda: stage3(CHUNKS - 1))
+        at(c, 3, finish3)
 
     each(CHUNKS, spectra)
-    each(middle + 2, stage4)
 
     def slot(c):
         grad(c)
-        at(c, 0, lambda: stage4(middle + 2))
-
-        @pl.when(c == jnp.where(last, 1, LATE))
-        def _():
-            stage4(CHUNKS - 1)
+        at(c, middle - 1, lambda: each(CHUNKS - 1, stage4))
 
     each(CHUNKS, slot)
 
-    theirs = xbuf.at[other]
+    theirs = xbuf.at[other, :, few]
     remote(theirs, theirs, x_s, x_r, (dp, other)).wait_recv()
+    theirs = vbuf.at[pl.ds(0, 2 * places - 1)]
+    remote(theirs, theirs, v_s, v_r, (dp, other)).wait_recv()
+    mine_x = xbuf.at[ctx, :, few]
+    remote(mine_x, mine_x, x_s, x_r, (dp, other)).wait_send()
+    xbuf[ctx, :, cols(tail)] = summed(ctx)
+    xbuf[other, :, cols(theirs_tail)] = summed(other)
     fbuf[...] = (xbuf[0].astype(f32) + xbuf[1].astype(f32)) * scale
 
     def sent(ref, sem):
@@ -380,8 +444,8 @@
 
     sent(csrc, c_s)
     sent(ysrc, y_s)
-    sent(zsrc.at[pl.ds(0, places - 1)], z_s)
-    sent(xbuf.at[ctx], x_s)
+    sent(zsrc.at[pl.ds(0, places - 1), :, few], z_s)
+    sent(vbuf.at[pl.ds(0, 2 * places - 1)], v_s)
     sent(taps_all.at[pl.ds(0, places - 1)], tz_s)
     sent(taps_all.at[pl.ds(0, places)], ty_s)
     sent(taps_all.at[pl.ds(0, pairs)], tc_s)
@@ -439,9 +503,10 @@
             vmem((places, count, channels), bf),
             vmem((places, count, channels), bf),
             vmem((ranks, count, channels), bf),
-            dma((CHUNKS,)), dma, dma, dma, pltpu.SemaphoreType.REGULAR,
+            vmem((2 * places, count, wide), bf),
+            dma((CHUNKS,)), dma, dma, dma, pltpu.SemaphoreType.REGULAR, pltpu.SemaphoreType.REGULAR,
             dma, dma((CHUNKS,)), dma, dma((places,)), dma, dma((places,)), dma, dma,
-            dma, dma((CHUNKS,)), dma, dma((CHUNKS,)), dma, dma((CHUNKS,)), dma, dma,
+            dma, dma((CHUNKS,)), dma, dma((CHUNKS,)), dma, dma((CHUNKS,)), dma, dma, dma, dma,
         ],
         compiler_params=pltpu.CompilerParams(
             collective_id=0, has_side_effects=True, vmem_limit_bytes=48_000_000

time: 31.9 us -> 30.9 us (0.969)
  the two profiles are of different devices: /device:TPU:0 before, /device:TPU:1 now
where the time goes in v5:
time: 30.9 us; the launch traced here: 30.8 us
  Pallas kernels  30.1 us (97%)
  between operations  0.64 us (2%)
    pallas_call x1, Pallas kernels, shards(): pl.pallas_call(functools.partial(kernel, pairs, scale), out_shape=(vmem((...  29.1 us
    pallas_call x1, Pallas kernels, store(): pl.pallas_call(body, out_shape=(jax.ShapeDtypeStruct((1, rows, channels),...  1.08 us

profile of v5, /device:TPU:1, one launch (start us, length us, event | category | flops | bytes accessed | tf_op | source)
XLA Modules:
  0.0 30.8 jit_solution(12198418179409140372)
XLA Ops:
  0.6 29.1 %shard_map.68 = (bf16[128,4096]{1,0:T(8,128)(2,1)S(1)}, f32[8,4096]{1,0:T(8,128)S(1)}) custom-call(bf16[128,4096]{1,0:T(8,128)(2,1)} %bitcast.3, bf16[128,4096]{1,0:T(8,128)(2,1)} %bitcast.4, bf16[128,4096]{1,0:T(8,128)(2,1)} %bitcast.5, bf16[8,4096]{1,0:T(8,128)(2,1)} %taps_hbm.1, bf16[3,256,256]{2,1,0:T(8,128)(2,1)} %constant.2.clone.f_hbm), custom_call_target="tpu_custom_call" | custom-call | tf_op jit(solution)/shard_map/pallas_call | solution.py:481
  29.7 1.1 %shard_map.69 = (bf16[1,128,4096]{2,1,0:T(8,128)(2,1)}, f32[8,4096]{1,0:T(8,128)}) custom-call(bf16[128,4096]{1,0:T(8,128)(2,1)S(1)} %get-tuple-element.4.g_ref, f32[8,4096]{1,0:T(8,128)S(1)} %get-tuple-element.5.f_ref), custom_call_target="tpu_custom_call" | custom-call | tf_op jit(solution)/shard_map/pallas_call | solution.py:540

commit v6 on v5

--- a/solution.py
+++ b/solution.py
@@ -65,6 +65,7 @@
 
 CHUNKS = 8
 EARLY = 2
+FIRST = 4
 MESH = pl.DeviceIdType.MESH
 
 
@@ -111,8 +112,8 @@
     load_in = local(in_hbm, x_in, ld_in)
 
     def loads(c):
-        local(cot_hbm.at[:, cols(c)], x_gc.at[0, :, cols(c)], ld_gc.at[c]).start()
-        local(gate_hbm.at[:, cols(c)], x_gc.at[1, :, cols(c)], ld_gc.at[c]).start()
+        local(cot_hbm.at[:, cols(c)], x_gc.at[0, :, cols(c)], ld_gc.at[lax.min(c, 1)]).start()
+        local(gate_hbm.at[:, cols(c)], x_gc.at[1, :, cols(c)], ld_gc.at[lax.min(c, 1)]).start()
 
     each(CHUNKS, loads)
 
@@ -144,17 +145,22 @@
         return remote(in_hbm.at[:, cols(c)], inc.at[:, cols(c)], inc_s, inc_r.at[c], (dp, other))
 
     def mix(c):
-        both = x_gc.at[:, :, cols(c)]
-        local(both, both, ld_gc.at[c]).wait()
         a = x_gc[0, :, cols(c)].astype(f32)
         b = x_gc[1, :, cols(c)].astype(f32)
         g[:, cols(c)] = (a * b).astype(bf)
 
-        @pl.when(jnp.logical_and(last, jnp.logical_or(core == 0, c < middle)))
+        @pl.when(jnp.logical_and(last, jnp.logical_or(core == 0, c < FIRST)))
         def _():
             rim(c).start()
 
-    each(CHUNKS, mix)
+    def loaded(at, k):
+        both = x_gc.at[:, :, at]
+        local(both, both, ld_gc.at[k]).wait()
+
+    loaded(pl.ds(0, wide), 0)
+    mix(jnp.int32(0))
+    loaded(pl.ds(wide, channels - wide), 1)
+    each(CHUNKS, mix, 1)
 
     @pl.when(first)
     def _():
@@ -401,7 +407,7 @@
 
         @pl.when(jnp.logical_and(i == CHUNKS - 1, jnp.logical_and(last, core == 1)))
         def _():
-            each(CHUNKS, lambda c: rim(c).start(), middle)
+            each(CHUNKS, lambda c: rim(c).start(), FIRST)
 
         @pl.when(i < CHUNKS - 1)
         def _():
@@ -504,7 +510,7 @@
             vmem((places, count, channels), bf),
             vmem((ranks, count, channels), bf),
             vmem((2 * places, count, wide), bf),
-            dma((CHUNKS,)), dma, dma, dma, pltpu.SemaphoreType.REGULAR, pltpu.SemaphoreType.REGULAR,
+            dma((2,)), dma, dma, dma, pltpu.SemaphoreType.REGULAR, pltpu.SemaphoreType.REGULAR,
             dma, dma((CHUNKS,)), dma, dma((places,)), dma, dma((places,)), dma, dma,
             dma, dma((CHUNKS,)), dma, dma((CHUNKS,)), dma, dma((CHUNKS,)), dma, dma, dma, dma,
         ],
@@ -518,7 +524,7 @@
     return store(out, fgrad)
 
 
-PARTS = 8
+PARTS = 1
 
 
 def store(grad, fgrad):

time: 30.9 us -> 30.8 us (level)
  no operation moved by 1% of the time
where the time goes in v6:
time: 30.8 us; the launch traced here: 30.7 us
  Pallas kernels  30 us (97%)
  between operations  0.64 us (2%)
    pallas_call x1, Pallas kernels, shards(): pl.pallas_call(functools.partial(kernel, pairs, scale), out_shape=(vmem((...  29 us
    pallas_call x1, Pallas kernels, store(): pl.pallas_call(body, out_shape=(jax.ShapeDtypeStruct((1, rows, channels),...  1.02 us

profile of v6, /device:TPU:1, one launch (start us, length us, event | category | flops | bytes accessed | tf_op | source)
XLA Modules:
  0.0 30.7 jit_solution(14052398038234384310)
XLA Ops:
  0.6 29.0 %shard_map.68 = (bf16[128,4096]{1,0:T(8,128)(2,1)S(1)}, f32[8,4096]{1,0:T(8,128)S(1)}) custom-call(bf16[128,4096]{1,0:T(8,128)(2,1)} %bitcast.3, bf16[128,4096]{1,0:T(8,128)(2,1)} %bitcast.4, bf16[128,4096]{1,0:T(8,128)(2,1)} %bitcast.5, bf16[8,4096]{1,0:T(8,128)(2,1)} %taps_hbm.1, bf16[3,256,256]{2,1,0:T(8,128)(2,1)} %constant.2.clone.f_hbm), custom_call_target="tpu_custom_call" | custom-call | tf_op jit(solution)/shard_map/pallas_call | solution.py:487
  29.6 1.0 %shard_map.69 = (bf16[1,128,4096]{2,1,0:T(8,128)(2,1)}, f32[8,4096]{1,0:T(8,128)}) custom-call(bf16[128,4096]{1,0:T(8,128)(2,1)S(1)} %get-tuple-element.4.g_ref, f32[8,4096]{1,0:T(8,128)S(1)} %get-tuple-element.5.f_ref), custom_call_target="tpu_custom_call" | custom-call | tf_op jit(solution)/shard_map/pallas_call | solution.py:546

commit v7 on v6

--- a/solution.py
+++ b/solution.py
@@ -275,7 +275,10 @@
         for k in range(1, places):
             total = total + zbuf[z_peer(k), :, cols(c)].astype(f32)
         xbuf[ctx, :, cols(c)] = total.astype(bf)
-        swap(c).start()
+
+        @pl.when(first)
+        def _():
+            swap(c).start()
 
     tail = chunk(CHUNKS - 1)
     theirs_tail = jnp.where(last, middle - 1, CHUNKS - 1)
@@ -429,9 +432,15 @@
 
     each(CHUNKS, spectra)
 
+    def swap_rest():
+        @pl.when(last)
+        def _():
+            block = xbuf.at[ctx, :, few]
+            remote(block, block, x_s, x_r, (dp, other)).start()
+
     def slot(c):
         grad(c)
-        at(c, middle - 1, lambda: each(CHUNKS - 1, stage4))
+        at(c, middle - 1, lambda: each(CHUNKS - 1, stage4), swap_rest)
 
     each(CHUNKS, slot)
 

time: 30.8 us -> 31 us (level)
  the two profiles are of different devices: /device:TPU:1 before, /device:TPU:0 now
where the time goes in v7:
time: 31 us; the launch traced here: 30.8 us
  Pallas kernels  30.2 us (97%)
  between operations  0.64 us (2%)
    pallas_call x1, Pallas kernels, shards(): pl.pallas_call(functools.partial(kernel, pairs, scale), out_shape=(vmem((...  29.1 us
    pallas_call x1, Pallas kernels, store(): pl.pallas_call(body, out_shape=(jax.ShapeDtypeStruct((1, rows, channels),...  1.02 us

profile of v7, /device:TPU:0, one launch (start us, length us, event | category | flops | bytes accessed | tf_op | source)
XLA Modules:
  0.0 30.8 jit_solution(7716753223164091963)
XLA Ops:
  0.6 29.1 %shard_map.68 = (bf16[128,4096]{1,0:T(8,128)(2,1)S(1)}, f32[8,4096]{1,0:T(8,128)S(1)}) custom-call(bf16[128,4096]{1,0:T(8,128)(2,1)} %bitcast.3, bf16[128,4096]{1,0:T(8,128)(2,1)} %bitcast.4, bf16[128,4096]{1,0:T(8,128)(2,1)} %bitcast.5, bf16[8,4096]{1,0:T(8,128)(2,1)} %taps_hbm.1, bf16[3,256,256]{2,1,0:T(8,128)(2,1)} %constant.2.clone.f_hbm), custom_call_target="tpu_custom_call" | custom-call | tf_op jit(solution)/shard_map/pallas_call | solution.py:496
  29.8 1.0 %shard_map.69 = (bf16[1,128,4096]{2,1,0:T(8,128)(2,1)}, f32[8,4096]{1,0:T(8,128)}) custom-call(bf16[128,4096]{1,0:T(8,128)(2,1)S(1)} %get-tuple-element.4.g_ref, f32[8,4096]{1,0:T(8,128)S(1)} %get-tuple-element.5.f_ref), custom_call_target="tpu_custom_call" | custom-call | tf_op jit(solution)/shard_map/pallas_call | solution.py:555
